TPU v7x, 256 devices: a whole 4x4x8 slice. The times are simulated.
256 devices in a mesh: snap: 32 (over z_hi, x, y), vert: 8 (over z_lo, core).
Axes of the slice: x: 4, y: 4, z: 8 (z_hi: 2, z_lo: 4; z = z_hi * 4 + z_lo), core: 2. Of those that a mesh axis runs over, the one named last changes fastest.
Arguments:
- features: bfloat16 [64, 8192, 128], P('snap', 'vert'), may hold values from -6 to 6
- tile_cols: int32 [64, 64, 8], P('snap', 'vert'), may hold values from 0 to 63
- tile_weights: int32 [64, 64, 8, 128, 128], P('snap', 'vert'), may hold values from 0 to 3
- graph_gain: float32 [2, 128], replicated, may hold values from 0.5 to 1.5
- graph_up: bfloat16 [2, 128, 512], replicated, may hold values from -0.5 to 0.5
- graph_down: bfloat16 [2, 512, 128], replicated, may hold values from -0.25 to 0.25
- lag_mix: float32 [2, 8, 128], replicated, may hold values from -2 to 2
- time_gain: float32 [2, 128], replicated, may hold values from 0.5 to 1.5
- time_up: bfloat16 [2, 128, 1024], replicated, may hold values from -0.5 to 0.5
- time_down: bfloat16 [2, 1024, 128], replicated, may hold values from -0.1875 to 0.1875
Outputs:
- result: bfloat16 [64, 8192, 128], P('snap', 'vert')
All inputs are finite; a program needn't handle non-finite values.
Results may differ from a plain program's by a relative error of at most 0.0085.
Values may be sent and summed in bfloat16 or wider, within the bound.
No kernel may reach another device: no remote copies, remote signals or barrier semaphores. Data moves between devices by JAX's collectives and lax.ppermute only.
A program may use at most 64 MiB of HBM per device.

v0:
```python
import jax
import jax.numpy as jnp
from jax import lax
from jax.sharding import PartitionSpec as P

eps = 1e-06


def rms_scale(activation, gain_row):
    return (
        activation
        * lax.rsqrt(jnp.mean(activation * activation, axis=-1, keepdims=True) + eps)
        * gain_row
    )


def mlp_branch(residual, mixed_rows, gain_row, up_weight, down_weight):
    feature_width = residual.shape[-1]
    normed = rms_scale(mixed_rows, gain_row).astype(jnp.bfloat16).reshape(-1, feature_width)
    hidden = jax.nn.gelu(jnp.dot(normed, up_weight, preferred_element_type=jnp.float32)).astype(
        jnp.bfloat16
    )
    branch = jnp.dot(hidden, down_weight, preferred_element_type=jnp.float32).reshape(
        residual.shape
    )
    return (residual.astype(jnp.float32) + branch).astype(jnp.bfloat16)


def lagged(sequence, lag_rows, before, out_count):
    widened = sequence.astype(jnp.float32)
    running = jnp.zeros((out_count,) + sequence.shape[1:], jnp.float32)
    for lag_step in range(lag_rows.shape[0]):
        running = running + lag_rows[lag_step] * lax.slice_in_dim(
            widened, before - lag_step, before - lag_step + out_count, axis=0
        )
    return running


def aggregate(snapshot, columns, blocks):
    tile_size = blocks.shape[-1]
    feature_width = snapshot.shape[-1]
    stacked = snapshot.reshape(-1, tile_size, feature_width)
    picked = stacked[columns]
    product = jnp.einsum("rkij,rkjf->rif", blocks, picked, preferred_element_type=jnp.float32)
    return product.reshape(-1, feature_width)


def on_device(
    features,
    tile_cols,
    tile_weights,
    graph_gain,
    graph_up,
    graph_down,
    lag_mix,
    time_gain,
    time_up,
    time_down,
):
    blocks = tile_weights.astype(jnp.bfloat16)
    state = features
    owners = lax.axis_size("snap")
    snap_dev, vert_dev, feature_width = features.shape
    lag_count = lag_mix.shape[1]
    for layer_index in range(graph_up.shape[0]):
        gathered = lax.all_gather(state, "vert", axis=1, tiled=True)
        summed = jax.vmap(aggregate)(gathered, tile_cols, blocks)
        graph_out = mlp_branch(
            state, summed, graph_gain[layer_index], graph_up[layer_index], graph_down[layer_index]
        )
        grouped = graph_out.reshape(snap_dev, owners, vert_dev // owners, feature_width)
        owned_rows = lax.all_to_all(grouped, "snap", split_axis=1, concat_axis=0, tiled=True)
        padded = jnp.concatenate(
            [jnp.zeros((lag_count - 1,) + owned_rows.shape[1:], jnp.bfloat16), owned_rows], axis=0
        )
        mixed_rows = lagged(padded, lag_mix[layer_index], lag_count - 1, owned_rows.shape[0])
        finished = mlp_branch(
            owned_rows,
            mixed_rows,
            time_gain[layer_index],
            time_up[layer_index],
            time_down[layer_index],
        )
        state = lax.all_to_all(finished, "snap", split_axis=0, concat_axis=1, tiled=True).reshape(
            snap_dev, vert_dev, feature_width
        )
    return state


def solution(mesh):
    return jax.shard_map(
        on_device,
        mesh=mesh,
        in_specs=(
            P("snap", "vert", None),
            P("snap", "vert", None),
            P("snap", "vert", None, None, None),
            P(),
            P(),
            P(),
            P(),
            P(),
            P(),
            P(),
        ),
        out_specs=P("snap", "vert", None),
        check_vma=False,
    )
```

profile of v0, /device:TPU:33, one launch (start us, length us, event | category | flops | bytes accessed | tf_op | source)
XLA Modules:
  0.0 265.1 jit_solution(5932802984013628403)
XLA Ops:
  6.5 0.7 all-gather.3.cloned.1.call-update
  8.0 0.8 slice_bitcast_fusion.9
  8.8 56.0 %all-gather.3.cloned.1.call-done = bf16[2,8192,128]{2,1,0:T(8,128)(2,1)} async-done(((bf16[2,1024,128]{2,1,0:T(8,128)(2,1)}), bf16[2,8192,128]{2,1,0:T(8,128)(2,1)}) %all-gather.3.cloned.1.call-update) | async-done | bytes 4194320 | tf_op jit(solution)/shard_map/all_gather | solution.py:66
  64.8 5.3 %gather_fusion = bf16[128,128,128]{2,1,0:T(8,128)(2,1)} fusion(bf16[2,64,128,128]{3,2,1,0:T(8,128)(2,1)} %bitcast.150, s32[128]{0:T(128)S(1)} %reshape.226), kind=kCustom, calls=%fused_computation | custom fusion | bytes 8389632 | tf_op jit(solution)/shard_map/vmap()/gather | solution.py:43
  70.1 5.9 %multiply_reduce_fusion.3 = (f32[2,8,128]{2,1,0:T(8,128)S(1)}, f32[2,8,128,128]{2,3,1,0:T(8,128)S(1)}) fusion(bf16[2,8,8,128,128]{4,3,2,1,0:T(8,128)(2,1)} %bitcast.143, s32[2,8,8,128,128]{4,3,2,1,0:T(8,128)} %param.12), kind=kOutput, calls=%fused_computation.91 | convolution fusion | flops 539490304 | bytes 13639680 | tf_op jit(solution)/shard_map/vmap(rkij,rkjf->rif)/dot_general | solution.py:44
  76.4 1.4 fusion.23
  77.9 0.7 fusion.42
  78.6 0.9 copy.19
  79.5 10.4 %all-to-all-start = ((bf16[2,32,32,128]{3,2,0,1:T(8,128)(2,1)}), bf16[2,32,32,128]{3,2,0,1:T(8,128)(2,1)S(1)}, u32[]{:S(2)}, u32[]{:S(2)}) async-start(bf16[2,32,32,128]{3,2,0,1:T(8,128)(2,1)} %copy.19), calls=%async_computation | async-start | bytes 1048576 | tf_op jit(solution)/shard_map/all_to_all | solution.py:72
  90.1 20.2 %all-to-all-done = bf16[2,32,32,128]{3,2,0,1:T(8,128)(2,1)S(1)} async-done(((bf16[2,32,32,128]{3,2,0,1:T(8,128)(2,1)}), bf16[2,32,32,128]{3,2,0,1:T(8,128)(2,1)S(1)}, u32[]{:S(2)}, u32[]{:S(2)}) %all-to-all-start) | async-done | bytes 524320 | tf_op jit(solution)/shard_map/all_to_all | solution.py:72
  111.5 2.9 %fusion.7 = bf16[2048,1024]{1,0:T(8,128)(2,1)S(1)} fusion(bf16[2048,128]{1,0:T(8,128)(2,1)S(1)} %bitcast.161, bf16[2,128,1024]{2,1,0:T(8,128)(2,1)S(1)} %copy-done.6), kind=kOutput, calls=%fused_computation.11 | convolution fusion | flops 555745280 | bytes 4980736 | tf_op jit(solution)/shard_map/dot_general | solution.py:20
  114.4 1.3 fusion.47
  115.7 21.4 %all_to_all.66 = bf16[64,1,32,128]{3,2,1,0:T(8,128)(2,1)S(1)} all-to-all(bf16[64,1,32,128]{3,2,1,0:T(8,128)(2,1)S(1)} %fusion.47), channel_id=1, replica_groups=mesh['snap'=32,'vert'=8] {'snap'}, dimensions={0} | all-to-all | bytes 1048576 | tf_op jit(solution)/shard_map/all_to_all | solution.py:84
  137.1 0.8 copy.21
  137.9 48.4 %all-gather.5.cloned.1.call-done = bf16[2,8192,128]{2,1,0:T(8,128)(2,1)} async-done(((bf16[2,1024,128]{2,1,0:T(8,128)(2,1)}), bf16[2,8192,128]{2,1,0:T(8,128)(2,1)}) %all-gather.5.cloned.1.call-update) | async-done | bytes 4194320 | tf_op jit(solution)/shard_map/all_gather | solution.py:66
  186.3 5.3 %gather_fusion.1 = bf16[128,128,128]{2,1,0:T(8,128)(2,1)} fusion(bf16[2,64,128,128]{3,2,1,0:T(8,128)(2,1)} %bitcast.151, s32[128]{0:T(128)S(1)} %reshape.226), kind=kCustom, calls=%fused_computation.1 | custom fusion | bytes 8389632 | tf_op jit(solution)/shard_map/vmap()/gather | solution.py:43
  191.6 5.9 %multiply_reduce_fusion.1 = (f32[2,8,128]{2,1,0:T(8,128)S(1)}, f32[2,8,128,128]{2,3,1,0:T(8,128)S(1)}) fusion(bf16[2,8,8,128,128]{4,3,2,1,0:T(8,128)(2,1)} %bitcast.142, s32[2,8,8,128,128]{4,3,2,1,0:T(8,128)} %param.12), kind=kOutput, calls=%fused_computation.87 | convolution fusion | flops 539490304 | bytes 13639680 | tf_op jit(solution)/shard_map/vmap(rkij,rkjf->rif)/dot_general | solution.py:44
  197.9 1.4 fusion.31
  199.3 0.7 fusion.43
  200.1 30.6 %all_to_all.67 = bf16[2,32,32,128]{3,2,0,1:T(8,128)(2,1)S(1)} all-to-all(bf16[2,32,32,128]{3,2,0,1:T(8,128)(2,1)S(1)} %copy.22), channel_id=1, replica_groups=mesh['snap'=32,'vert'=8] {'snap'}, dimensions={1} | all-to-all | bytes 1048576 | tf_op jit(solution)/shard_map/all_to_all | solution.py:72
  231.8 2.9 %fusion.15 = bf16[2048,1024]{1,0:T(8,128)(2,1)S(1)} fusion(bf16[2048,128]{1,0:T(8,128)(2,1)S(1)} %bitcast.163, bf16[2,128,1024]{2,1,0:T(8,128)(2,1)S(1)} %copy-done.6), kind=kOutput, calls=%fused_computation.19 | convolution fusion | flops 555745280 | bytes 4980736 | tf_op jit(solution)/shard_map/dot_general | solution.py:20
  234.8 1.3 fusion.46
  236.0 21.4 %all_to_all.68 = bf16[64,1,32,128]{3,2,1,0:T(8,128)(2,1)S(1)} all-to-all(bf16[64,1,32,128]{3,2,1,0:T(8,128)(2,1)S(1)} %fusion.46), channel_id=1, replica_groups=mesh['snap'=32,'vert'=8] {'snap'}, dimensions={0} | all-to-all | bytes 1048576 | tf_op jit(solution)/shard_map/all_to_all | solution.py:84
  257.4 0.8 copy.24
  (36 shorter events, 3.9 us)
Async XLA Ops:
  6.5 58.3 %all-gather.3.cloned.1.call-start = ((), (), s32[]{:S(2)}) async-start(), calls=%async_computation.4 | async-start | bytes 4718592 | tf_op jit(solution)/shard_map/all_gather | solution.py:66
  70.1 6.3 %copy-start.7 = (bf16[2,128,512]{2,1,0:T(8,128)(2,1)S(1)}, bf16[2,128,512]{2,1,0:T(8,128)(2,1)}, u32[]{:S(2)}) copy-start(bf16[2,128,512]{2,1,0:T(8,128)(2,1)} %param.14) | copy-start | bytes 786436
  76.4 1.5 copy-start.1
  76.4 1.5 copy-start.3
  77.9 12.1 %copy-start.5 = (f32[2,128]{1,0:T(2,128)S(1)}, f32[2,128]{1,0:T(2,128)}, u32[]{:S(2)}) copy-start(f32[2,128]{1,0:T(2,128)} %param.17) | copy-start | bytes 3076
  77.9 12.1 %copy-start.4 = (f32[2,8,128]{2,1,0:T(8,128)S(1)}, f32[2,8,128]{2,1,0:T(8,128)}, u32[]{:S(2)}) copy-start(f32[2,8,128]{2,1,0:T(8,128)} %param.16) | copy-start | bytes 24580
  79.5 30.8 %all-to-all-start = ((bf16[2,32,32,128]{3,2,0,1:T(8,128)(2,1)}), bf16[2,32,32,128]{3,2,0,1:T(8,128)(2,1)S(1)}, u32[]{:S(2)}, u32[]{:S(2)}) async-start(bf16[2,32,32,128]{3,2,0,1:T(8,128)(2,1)} %copy.19), calls=%async_computation | async-start | bytes 1048576 | tf_op jit(solution)/shard_map/all_to_all | solution.py:72
  90.0 96.4 %all-gather.5.cloned.1.call-start = ((), (), s32[]{:S(2)}) async-start(), calls=%async_computation.5 | async-start | bytes 4718592 | tf_op jit(solution)/shard_map/all_gather | solution.py:66
  110.4 1.0 copy-start.6
  111.5 3.0 %copy-start.2 = (bf16[2,1024,128]{2,1,0:T(8,128)(2,1)S(1)}, bf16[2,1024,128]{2,1,0:T(8,128)(2,1)}, u32[]{:S(2)}) copy-start(bf16[2,1024,128]{2,1,0:T(8,128)(2,1)} %param.19) | copy-start | bytes 1572868
  197.9 1.5 copy-start
Sparse Core Ops, SparseCore 0:
  9.1 55.6 all-gather.2
  138.1 48.2 all-gather.4
where the time goes:
time: 266 us; the launch traced here: 265 us
  waiting for transfers between devices  125 us (47%)
  blocking collectives  73.3 us (28%)
  matrix products  24.5 us (9%)
  local copies, waits for them, and re-layouts  14 us (5%)
  between operations  13.7 us (5%)
  starting transfers between devices  10.5 us (4%)
  other arithmetic  3.68 us (1%)
    all_gather x2, waiting for transfers between devices, on_device(): gathered = lax.all_gather(state, 'vert', axis=1, tiled=True)  104 us
    all_to_all x2, blocking collectives, on_device(): lax.all_to_all(finished, 'snap', split_axis=0, concat_axis=1, tiled=True)  42.8 us
    all_to_all x1, blocking collectives, on_device(): lax.all_to_all(grouped, 'snap', split_axis=1, concat_axis=0, tiled=True)  30.6 us
    all_to_all x1, waiting for transfers between devices, on_device(): lax.all_to_all(grouped, 'snap', split_axis=1, concat_axis=0, tiled=True)  20.2 us
    dot_general x2, matrix products, aggregate(): jnp.einsum('rkij,rkjf->rif', blocks, picked, preferred_element_type=jnp.f...  11.8 us
    gather x3, local copies, waits for them, and re-layouts, aggregate(): picked = stacked[columns]  10.6 us
    all_to_all x1, starting transfers between devices, on_device(): lax.all_to_all(grouped, 'snap', split_axis=1, concat_axis=0, tiled=True)  10.4 us
    dot_general x4, matrix products, mlp_branch(): jnp.dot(normed, up_weight, preferred_element_type=jnp.float32)  8.74 us
  transfers between devices with their start and end apart: 3, of which 3 were waited for; matrix products, arithmetic and copies ran while one was open for 1% of the time, Pallas kernels for 0%

commit v1 on v0

--- a/solution.py
+++ b/solution.py
@@ -63,7 +63,9 @@
     snap_dev, vert_dev, feature_width = features.shape
     lag_count = lag_mix.shape[1]
     for layer_index in range(graph_up.shape[0]):
-        gathered = lax.all_gather(state, "vert", axis=1, tiled=True)
+        gathered = jnp.concatenate(
+            lax.all_to_all(jnp.stack([state] * lax.axis_size("vert")), "vert", 0, 0), axis=1
+        )
         summed = jax.vmap(aggregate)(gathered, tile_cols, blocks)
         graph_out = mlp_branch(
             state, summed, graph_gain[layer_index], graph_up[layer_index], graph_down[layer_index]

time: 266 us -> 347 us (1.30)
  the two profiles are of different devices: /device:TPU:33 before, /device:TPU:32 now
where the time goes in v1:
time: 347 us; the launch traced here: 346 us
  blocking collectives  167 us (48%)
  waiting for transfers between devices  108 us (31%)
  matrix products  24.5 us (7%)
  local copies, waits for them, and re-layouts  23.9 us (7%)
  starting transfers between devices  18.6 us (5%)
    all_to_all x1, blocking collectives, on_device(): lax.all_to_all(jnp.stack([state] * lax.axis_size('vert')), 'vert', 0, 0)  99.9 us
    all_to_all x1, waiting for transfers between devices, on_device(): lax.all_to_all(jnp.stack([state] * lax.axis_size('vert')), 'vert', 0, 0)  90.4 us
    all_to_all x2, blocking collectives, on_device(): lax.all_to_all(finished, 'snap', split_axis=0, concat_axis=1, tiled=True)  40.2 us
    all_to_all x1, blocking collectives, on_device(): lax.all_to_all(grouped, 'snap', split_axis=1, concat_axis=0, tiled=True)  27.4 us
    all_to_all x1, waiting for transfers between devices, on_device(): lax.all_to_all(grouped, 'snap', split_axis=1, concat_axis=0, tiled=True)  18 us
    all_to_all x1, starting transfers between devices, on_device(): lax.all_to_all(grouped, 'snap', split_axis=1, concat_axis=0, tiled=True)  12.2 us
    dot_general x2, matrix products, aggregate(): jnp.einsum('rkij,rkjf->rif', blocks, picked, preferred_element_type=jnp.f...  11.8 us
    gather x3, local copies, waits for them, and re-layouts, aggregate(): picked = stacked[columns]  10.6 us
  transfers between devices with their start and end apart: 2, of which 2 were waited for; matrix products, arithmetic and copies ran while one was open for 0% of the time, Pallas kernels for 0%

profile of v1, /device:TPU:32, one launch (start us, length us, event | category | flops | bytes accessed | tf_op | source)
XLA Modules:
  0.0 346.2 jit_solution(81291726882593230)
XLA Ops:
  0.0 3.8 %stack.4 = bf16[8,2,1024,128]{3,2,1,0:T(8,128)(2,1)} broadcast(bf16[2,1024,128]{2,1,0:T(8,128)(2,1)} %param.10), dimensions={1,2,3} | broadcast | bytes 4718592 | tf_op jit(solution)/shard_map/stack | solution.py:67
  3.8 6.4 %all-to-all-start = ((bf16[8,2,1024,128]{3,2,1,0:T(8,128)(2,1)}), bf16[8,2,1024,128]{3,2,1,0:T(8,128)(2,1)}, u32[]{:S(2)}, u32[]{:S(2)}) async-start(bf16[8,2,1024,128]{3,2,1,0:T(8,128)(2,1)} %stack.4), calls=%async_computation | async-start | bytes 8388608 | tf_op jit(solution)/shard_map/all_to_all | solution.py:67
  10.4 90.4 %all-to-all-done = bf16[8,2,1024,128]{3,2,1,0:T(8,128)(2,1)} async-done(((bf16[8,2,1024,128]{3,2,1,0:T(8,128)(2,1)}), bf16[8,2,1024,128]{3,2,1,0:T(8,128)(2,1)}, u32[]{:S(2)}, u32[]{:S(2)}) %all-to-all-start) | async-done | bytes 4194336 | tf_op jit(solution)/shard_map/all_to_all | solution.py:67
  100.8 4.6 %copy.19 = bf16[8,2,1024,128]{3,2,0,1:T(8,128)(2,1)} copy(bf16[8,2,1024,128]{3,2,1,0:T(8,128)(2,1)} %all-to-all-done) | data formatting | bytes 8388608 | tf_op jit(solution)/shard_map/all_to_all | solution.py:67
  105.4 5.2 %gather_fusion = bf16[128,128,128]{2,1,0:T(8,128)(2,1)} fusion(bf16[2,64,128,128]{3,2,1,0:T(8,128)(2,1)} %bitcast.149, s32[128]{0:T(128)S(1)} %reshape.231), kind=kCustom, calls=%fused_computation | custom fusion | bytes 8389632 | tf_op jit(solution)/shard_map/vmap()/gather | solution.py:43
  110.6 5.9 %multiply_reduce_fusion.3 = (f32[2,8,128]{2,1,0:T(8,128)S(1)}, f32[2,8,128,128]{2,3,1,0:T(8,128)S(1)}) fusion(bf16[2,8,8,128,128]{4,3,2,1,0:T(8,128)(2,1)} %bitcast.147, s32[2,8,8,128,128]{4,3,2,1,0:T(8,128)} %param.12), kind=kOutput, calls=%fused_computation.91 | convolution fusion | flops 539490304 | bytes 13639680 | tf_op jit(solution)/shard_map/vmap(rkij,rkjf->rif)/dot_general | solution.py:44
  116.9 1.4 fusion.23
  119.1 0.9 copy.20
  120.0 12.2 %all-to-all-start.1 = ((bf16[2,32,32,128]{3,2,0,1:T(8,128)(2,1)}), bf16[2,32,32,128]{3,2,0,1:T(8,128)(2,1)S(1)}, u32[]{:S(2)}, u32[]{:S(2)}) async-start(bf16[2,32,32,128]{3,2,0,1:T(8,128)(2,1)} %copy.20), calls=%async_computation.1 | async-start | bytes 1048576 | tf_op jit(solution)/shard_map/all_to_all | solution.py:74
  132.3 18.0 %all-to-all-done.1 = bf16[2,32,32,128]{3,2,0,1:T(8,128)(2,1)S(1)} async-done(((bf16[2,32,32,128]{3,2,0,1:T(8,128)(2,1)}), bf16[2,32,32,128]{3,2,0,1:T(8,128)(2,1)S(1)}, u32[]{:S(2)}, u32[]{:S(2)}) %all-to-all-start.1) | async-done | bytes 524320 | tf_op jit(solution)/shard_map/all_to_all | solution.py:74
  151.5 2.9 fusion.7
  154.4 1.3 fusion.47
  155.7 18.7 %all_to_all.76 = bf16[64,1,32,128]{3,2,1,0:T(8,128)(2,1)S(1)} all-to-all(bf16[64,1,32,128]{3,2,1,0:T(8,128)(2,1)S(1)} %fusion.47), channel_id=1, replica_groups=mesh['snap'=32,'vert'=8] {'snap'}, dimensions={0} | all-to-all | bytes 1048576 | tf_op jit(solution)/shard_map/all_to_all | solution.py:86
  174.5 0.8 stack.5
  175.3 99.9 %all_to_all.77 = bf16[8,2,1024,128]{3,2,1,0:T(8,128)(2,1)S(1)} all-to-all(bf16[8,2,1024,128]{3,2,1,0:T(8,128)(2,1)S(1)} %stack.5), channel_id=1, replica_groups=mesh['snap'=32,'vert'=8] {'vert'}, dimensions={0} | all-to-all | bytes 8388608 | tf_op jit(solution)/shard_map/all_to_all | solution.py:67
  275.2 2.2 copy.23
  277.4 5.3 %gather_fusion.1 = bf16[128,128,128]{2,1,0:T(8,128)(2,1)} fusion(bf16[2,64,128,128]{3,2,1,0:T(8,128)(2,1)} %bitcast.148, s32[128]{0:T(128)S(1)} %reshape.231), kind=kCustom, calls=%fused_computation.1 | custom fusion | bytes 8389632 | tf_op jit(solution)/shard_map/vmap()/gather | solution.py:43
  282.7 5.9 %multiply_reduce_fusion.1 = (f32[2,8,128]{2,1,0:T(8,128)S(1)}, f32[2,8,128,128]{2,3,1,0:T(8,128)S(1)}) fusion(bf16[2,8,8,128,128]{4,3,2,1,0:T(8,128)(2,1)} %bitcast.146, s32[2,8,8,128,128]{4,3,2,1,0:T(8,128)} %param.12), kind=kOutput, calls=%fused_computation.87 | convolution fusion | flops 539490304 | bytes 13639680 | tf_op jit(solution)/shard_map/vmap(rkij,rkjf->rif)/dot_general | solution.py:44
  289.0 1.4 fusion.31
  291.2 27.4 %all_to_all.78 = bf16[2,32,32,128]{3,2,0,1:T(8,128)(2,1)S(1)} all-to-all(bf16[2,32,32,128]{3,2,0,1:T(8,128)(2,1)S(1)} %copy.24), channel_id=1, replica_groups=mesh['snap'=32,'vert'=8] {'snap'}, dimensions={1} | all-to-all | bytes 1048576 | tf_op jit(solution)/shard_map/all_to_all | solution.py:74
  319.7 2.9 fusion.15
  322.6 1.3 fusion.46
  323.9 21.4 %all_to_all.79 = bf16[64,1,32,128]{3,2,1,0:T(8,128)(2,1)S(1)} all-to-all(bf16[64,1,32,128]{3,2,1,0:T(8,128)(2,1)S(1)} %fusion.46), channel_id=1, replica_groups=mesh['snap'=32,'vert'=8] {'snap'}, dimensions={0} | all-to-all | bytes 1048576 | tf_op jit(solution)/shard_map/all_to_all | solution.py:86
  345.4 0.8 copy.26
  (39 shorter events, 4.6 us)
Async XLA Ops:
  3.8 6.4 %copy-start.3 = (s32[2,8,8]{2,1,0:T(8,128)S(1)}, s32[2,8,8]{2,1,0:T(8,128)}, u32[]{:S(2)}) copy-start(s32[2,8,8]{2,1,0:T(8,128)} %param.11) | copy-start | bytes 1540
  3.8 6.5 %copy-start.5 = (f32[2,128]{1,0:T(2,128)S(1)}, f32[2,128]{1,0:T(2,128)}, u32[]{:S(2)}) copy-start(f32[2,128]{1,0:T(2,128)} %param.13) | copy-start | bytes 3076
  3.8 96.9 %all-to-all-start = ((bf16[8,2,1024,128]{3,2,1,0:T(8,128)(2,1)}), bf16[8,2,1024,128]{3,2,1,0:T(8,128)(2,1)}, u32[]{:S(2)}, u32[]{:S(2)}) async-start(bf16[8,2,1024,128]{3,2,1,0:T(8,128)(2,1)} %stack.4), calls=%async_computation | async-start | bytes 8388608 | tf_op jit(solution)/shard_map/all_to_all | solution.py:67
  110.6 6.3 %copy-start.8 = (bf16[2,128,512]{2,1,0:T(8,128)(2,1)S(1)}, bf16[2,128,512]{2,1,0:T(8,128)(2,1)}, u32[]{:S(2)}) copy-start(bf16[2,128,512]{2,1,0:T(8,128)(2,1)} %param.14) | copy-start | bytes 786436
  116.9 1.5 copy-start
  116.9 1.5 copy-start.2
  118.4 13.8 %copy-start.6 = (f32[2,128]{1,0:T(2,128)S(1)}, f32[2,128]{1,0:T(2,128)}, u32[]{:S(2)}) copy-start(f32[2,128]{1,0:T(2,128)} %param.17) | copy-start | bytes 3076
  118.4 13.9 %copy-start.4 = (f32[2,8,128]{2,1,0:T(8,128)S(1)}, f32[2,8,128]{2,1,0:T(8,128)}, u32[]{:S(2)}) copy-start(f32[2,8,128]{2,1,0:T(8,128)} %param.16) | copy-start | bytes 24580
  120.0 30.3 %all-to-all-start.1 = ((bf16[2,32,32,128]{3,2,0,1:T(8,128)(2,1)}), bf16[2,32,32,128]{3,2,0,1:T(8,128)(2,1)S(1)}, u32[]{:S(2)}, u32[]{:S(2)}) async-start(bf16[2,32,32,128]{3,2,0,1:T(8,128)(2,1)} %copy.20), calls=%async_computation.1 | async-start | bytes 1048576 | tf_op jit(solution)/shard_map/all_to_all | solution.py:74
  150.4 1.0 copy-start.7
  151.5 2.9 copy-start.1
